TPU v7x, 256 devices: a whole 4x4x8 slice. The times are simulated.
256 devices in a mesh: row: 8 (over z), col: 8 (over x, core), sub: 4 (over y).
Axes of the slice: x: 4, y: 4, z: 8, core: 2. Of those that a mesh axis runs over, the one named last changes fastest.
Arguments:
- front_entries: float32 [8192, 8192], P('row', ('col', 'sub')), may hold values from -1 to 4, as said below
- child_blocks: float32 [4, 2048, 2048], P('sub', 'row', 'col'), may hold values from -1 to 2, as said below
- child_map: int32 [4, 16], P('sub'), may hold values from 0 to 63, as said below
Outputs:
- factored: float32 [8192, 8192], P('row', ('col', 'sub'))
Inputs may be any that keep to these rules, and one draw needn't show every extreme that they name: Each row of child_map lists 16 different parent blocks in increasing order and ends with block 63. In natural order front_entries is a symmetric matrix, and the assembled front is positive definite. `child_blocks`: in natural order each child's contribution block is a symmetric matrix.
All inputs are finite; a program needn't handle non-finite values.
Results may differ from a plain program's by a relative error of at most 0.00005.
Values sent between devices are 32-bit elements; how exact they have to be, the bound alone decides.
A program may use at most 128 MiB of HBM per device.

v0:
```python
import jax
import jax.numpy as jnp
from jax import lax
from jax.experimental import pallas as pl
from jax.experimental.pallas import tpu as pltpu
from jax.sharding import PartitionSpec as P

BLK = 128
NPIV = 6
PIV = NPIV * BLK
PLANE = ("col", "sub")
HI = lax.Precision.HIGHEST
VM = pl.BlockSpec(memory_space=pltpu.VMEM)
SM = pl.BlockSpec(memory_space=pltpu.SMEM)


def nt(a, b, precision=HI):
    return lax.dot_general(a, b, (((1,), (1,)), ((), ())), precision=precision, preferred_element_type=jnp.float32)
def tn(a, b, precision=HI):
    return lax.dot_general(a, b, (((0,), (0,)), ((), ())), precision=precision, preferred_element_type=jnp.float32)

def split(x):
    high = x.astype(jnp.bfloat16)
    return high, (x - high.astype(jnp.float32)).astype(jnp.bfloat16)


def dot3(a, b, dims):
    def one(x, y):
        return lax.dot_general(x, y, (dims, ((), ())), preferred_element_type=jnp.float32)

    return one(a[0], b[0]) + (one(a[0], b[1]) + one(a[1], b[0]))


def tn3(a, b):
    return dot3(split(a), split(b), ((0,), (0,)))


def nt3(a, b):
    return dot3(split(a), split(b), ((1,), (1,)))


def rsqrt(x):
    return lax.rsqrt(x)

def wide(x):
    return jnp.concatenate([x, x], axis=1)

def eliminate(a_ref):
    sub = lax.broadcasted_iota(jnp.int32, (8, 256), 0)
    ahead = []
    for g in range(16):
        if g == 0:
            ahead = [a_ref[8 * h : 8 * h + 8, :] for h in range(2 + 1)]
        elif g + 2 < 16:
            ahead.append(a_ref[8 * (g + 2) : 8 * (g + 2) + 8, :])
        rows = ahead.pop(0)
        left = rows[:, :BLK]
        e = {}
        for j in range(8):
            c = jnp.broadcast_to(left[:, 8 * g + j : 8 * g + j + 1], (8, BLK))
            for i in range(j, 8):
                e[j, i] = jnp.broadcast_to(c[i : i + 1, :], (8, BLK))
        r = [jnp.broadcast_to(rows[i : i + 1, :], (8, 256)) for i in range(8)]
        cols = [[jnp.broadcast_to(n[:, 8 * g + j : 8 * g + j + 1], (8, BLK)) for j in range(8)] for n in ahead]
        out = None
        for j in range(8):
            s = rsqrt(e[j, j])
            u = {i: e[j, i] * s for i in range(j + 1, 8)}
            for i in range(j + 1, 8):
                for m in range(i, 8):
                    e[i, m] = e[i, m] - u[i] * u[m]
            rj = r[j] * wide(s)
            for i in range(j + 1, 8):
                r[i] = r[i] - wide(u[i]) * rj
            for h in range(len(ahead)):
                cj = cols[h][j] * s
                for m in range(j + 1, 8):
                    cols[h][m] = cols[h][m] - cj * u[m]
                ahead[h] = ahead[h] - wide(cj) * rj
            out = rj if out is None else jnp.where(sub == j, rj, out)
        a_ref[8 * g : 8 * g + 8, :] = out
        low = 8 * (g + 1 + 2)
        if low < BLK:
            t = tn3(out[:, :BLK], out)
            a_ref[low:, :] = a_ref[low:, :] - t[low:, :]

def factor_begin(l_ref, m_ref):
    for i in range(NPIV - 1):
        m_ref[i * BLK : (i + 1) * BLK, (i + 1) * BLK :] = jnp.zeros((BLK, PIV - (i + 1) * BLK), jnp.float32)
    l_ref[...] = jnp.zeros_like(l_ref)


def diagonal(a_ref, block):
    r_iota = lax.broadcasted_iota(jnp.int32, (BLK, BLK), 0)
    c_iota = lax.broadcasted_iota(jnp.int32, (BLK, BLK), 1)
    a_ref[:, :BLK] = block
    a_ref[:, BLK:] = jnp.where(r_iota == c_iota, 1.0, 0.0)
    eliminate(a_ref)


def factor_finish(b, l_ref, y_ref, a_ref, m_ref):
    r_iota = lax.broadcasted_iota(jnp.int32, (BLK, BLK), 0)
    c_iota = lax.broadcasted_iota(jnp.int32, (BLK, BLK), 1)
    at = pl.ds(b * BLK if isinstance(b, int) else pl.multiple_of(b * BLK, BLK), BLK)
    y = a_ref[:, BLK:]
    y_ref[b] = y
    l_ref[at, at] = jnp.where(r_iota >= c_iota, a_ref[:, :BLK].T, 0.0)

    def solve(i, c):
        rows = pl.ds(pl.multiple_of(i * BLK, BLK), BLK)
        l_ref[rows, at] = nt(m_ref[rows, at], y)
        return c

    lax.fori_loop(b + 1, NPIV, solve, 0)

    def update(i, c):
        rows = pl.ds(pl.multiple_of(i * BLK, BLK), BLK)
        m_ref[rows, :] = m_ref[rows, :] - nt3(l_ref[rows, at], l_ref[:, at])
        return c

    lax.fori_loop(b + 1, NPIV, update, 0)


def factor_steps(l_ref, y_ref, a_ref, m_ref, progress):
    def step(b, carry):
        progress(b)
        at = pl.ds(pl.multiple_of(b * BLK, BLK), BLK)
        diagonal(a_ref, m_ref[at, at])
        factor_finish(b, l_ref, y_ref, a_ref, m_ref)
        return carry

    lax.fori_loop(1, NPIV, step, 0)


MESH = pl.DeviceIdType.MESH
TILES = [(i, j) for i in range(NPIV) for j in range(i + 1)]
NTILE = len(TILES)


class Place:
    def __init__(self):
        self.r, self.c, self.s = (lax.axis_index(a) for a in ("row", "col", "sub"))
        self.e = self.c * 4 + self.s
        self.core = self.c % 2
        self.chip = (self.c // 2) * 4 + self.s
        self.partner = (self.r, self.c + 1 - 2 * self.core, self.s)

    def plane(self, d):
        p = (self.e + d) % 32
        return p, (self.r, p // 4, p % 4)

    def same_core(self, d):
        p = (self.chip + d) % 16
        c = (p // 4) * 2 + self.core
        return c * 4 + p % 4, (self.r, c, p % 4)

    def line(self, d):
        return ((self.r + d) % 8, self.c, self.s)

    def greet(self, meanwhile):
        barrier = pltpu.get_barrier_semaphore()

        def plane(d, carry):
            pl.semaphore_signal(barrier, inc=1, device_id=self.plane(d)[1], device_id_type=MESH)
            return carry

        def line(d, carry):
            pl.semaphore_signal(barrier, inc=1, device_id=self.line(d), device_id_type=MESH)
            return carry

        lax.fori_loop(1, 32, plane, 0)
        lax.fori_loop(1, 8, line, 0)
        meanwhile()
        pl.semaphore_wait(barrier, 38)


def push(src, dst, ssem, rsem, device):
    return pltpu.make_async_remote_copy(
        src_ref=src, dst_ref=dst, send_sem=ssem, recv_sem=rsem, device_id=device, device_id_type=MESH
    )


def arrive(ref, sem):
    pltpu.make_async_copy(ref, ref, sem).wait()


def loop(low, high, f):
    def one(d, carry):
        f(d)
        return carry

    lax.fori_loop(low, high, one, 0)


def gather_kernel(
    tile_ref, whole_ref, list_ref, k_ref, maps_ref, buf_ref, panel_ref, first_ref,
    child_ref, strip_ref, front_ref, map_ref, z_ref, acc_ref, send, got, z_got, f_got, k_got, p_got, ring_got,
):
    at = Place()
    r, c, s, e = at.r, at.c, at.s, at.e
    has_front = (c < NPIV) & (s == 0)

    def prepare():
        fetch = pltpu.make_async_copy(whole_ref.at[:, pl.ds(0, BLK)], strip_ref, got.at[5])
        fetch.start()
        for i in range(2):
            for j in range(2):
                child_ref[:, i, j] = tile_ref[0, i * BLK : (i + 1) * BLK, j * BLK : (j + 1) * BLK].reshape(32, 4, BLK)
        for i in range(16):
            map_ref[i : i + 1, :] = jnp.full((1, BLK), list_ref[0, i], jnp.int32)
        for i in range(NPIV - 1):
            z_ref[i, 4 * (i + 1) : 24] = jnp.zeros((20 - 4 * i, 4, BLK), jnp.float32)
        fetch.wait()

        @pl.when(has_front)
        def _():
            for i in range(8):
                front_ref[i] = strip_ref[i * BLK : (i + 1) * BLK, :].reshape(32, 4, BLK)

    at.greet(prepare)
    seat = jnp.minimum(c, NPIV - 1)

    def child_copy(d):
        p, device = at.plane(d)
        return push(child_ref.at[p], buf_ref.at[r, e], send.at[0], got.at[0], device)

    def front_copy(d):
        p, device = at.plane(d)
        return push(front_ref.at[0, p], panel_ref.at[seat, 0], send.at[1], got.at[1], device)

    def rest_copy(d):
        p, device = at.plane(d)
        return push(front_ref.at[pl.ds(1, 7), p], panel_ref.at[seat, pl.ds(1, 7)], send.at[4], got.at[4], device)

    def map_copy(d):
        return push(map_ref, maps_ref.at[s], send.at[2], got.at[2], (r, c, (s + d) % 4))

    pltpu.make_async_copy(child_ref.at[e], buf_ref.at[r, e], got.at[0]).start()
    pltpu.make_async_copy(map_ref, maps_ref.at[s], got.at[2]).start()
    loop(1, 32, lambda d: child_copy(d).start())

    @pl.when(has_front)
    def _():
        pltpu.make_async_copy(front_ref.at[0, e], panel_ref.at[seat, 0], got.at[1]).start()
        loop(1, 32, lambda d: front_copy(d).start())

    for d in range(1, 4):
        map_copy(d).start()

    def z_copies(i, d):
        device = at.line(d)
        tiles, own = pl.ds(0, 4 * (i + 1)), pl.ds(0, i + 1)
        return (
            push(buf_ref.at[i, tiles, 0, 0], z_ref.at[i, tiles], send.at[3], z_got.at[i], device),
            push(panel_ref.at[own, 0], z_ref.at[i, pl.ds(24, i + 1)], send.at[3], f_got.at[i], device),
        )

    def ring_copy(way, k, h):
        block = (r + 8 - k) % 8 if way == 0 else (r + k) % 8
        half = buf_ref.at[block, :, h]
        return push(half, half, send.at[5 + way], ring_got.at[way, 2 * k + h], at.line(1 if way == 0 else 7))

    def ring_wait(way, k, h):
        block = (r + 7 - k) % 8 if way == 0 else (r + 1 + k) % 8
        arrive(buf_ref.at[block, :, h], ring_got.at[way, 2 * k + h])

    hops = [(way, k, h) for k in range(4) for h in range(2) for way in range(2) if k < 3 or h == way]

    def ring_step(k):
        for hop in hops:
            if hop[1] == k:
                if k:
                    ring_wait(hop[0], k - 1, hop[2])
                ring_copy(*hop).start()

    arrive(buf_ref.at[r], got.at[0])
    arrive(panel_ref.at[:, 0], got.at[1])

    for i in range(NPIV):
        @pl.when(r == i)
        def _():
            tiles, own = pl.ds(0, 4 * (i + 1)), pl.ds(0, i + 1)
            pltpu.make_async_copy(buf_ref.at[i, tiles, 0, 0], z_ref.at[i, tiles], z_got.at[i]).start()
            pltpu.make_async_copy(panel_ref.at[own, 0], z_ref.at[i, pl.ds(24, i + 1)], f_got.at[i]).start()
            for d in (4, 3, 5, 2, 6, 1, 7):
                for copy in z_copies(i, d):
                    copy.start()

    @pl.when(has_front)
    def _():
        pltpu.make_async_copy(front_ref.at[pl.ds(1, 7), e], panel_ref.at[seat, pl.ds(1, 7)], got.at[4]).start()
        loop(1, 32, lambda d: rest_copy(d).start())

    ring_step(0)
    arrive(maps_ref, got.at[2])
    for i in range(NPIV):
        arrive(z_ref.at[i, pl.ds(0, 4 * (i + 1))], z_got.at[i])
        arrive(z_ref.at[i, pl.ds(24, i + 1)], f_got.at[i])

    for t, (i, j) in enumerate(TILES):
        acc_ref[t] = z_ref[i, 24 + j]

    def add_child(q):
        wanted = maps_ref[q][:NPIV]
        strips = []
        for j in range(NPIV):
            strip = None
            for seat_j in range(j + 1):
                pick = jnp.where(wanted[seat_j : seat_j + 1] == j, 1.0, 0.0)[None]
                term = z_ref[:, seat_j * 4 + q] * pick
                strip = term if strip is None else strip + term
            strips.append(strip)
        for j in range(NPIV):
            for i in range(j, NPIV):
                pick = jnp.where(wanted == i, 1.0, 0.0)[:, None, :]
                acc_ref[i * (i + 1) // 2 + j] += jnp.sum(strips[j] * pick, axis=0)

    loop(0, 4, add_child)

    own_k = pltpu.make_async_copy(acc_ref, k_ref.at[:, e], got.at[3])
    own_k.start()

    def k_copy(d):
        return push(acc_ref, k_ref.at[:, e], send.at[7], k_got.at[d], at.same_core(d)[1])

    def pair_copy(d):
        where_e = at.same_core(16 - d)[0]
        return push(k_ref.at[:, where_e], k_ref.at[:, where_e], send.at[8], p_got.at[d], at.partner)

    def forward(d):
        k_copy(d).wait_recv()
        pair_copy(d).start()

    loop(1, 16, lambda d: k_copy(d).start())
    ring_step(1)
    own_k.wait()
    pair_copy(0).start()
    ring_step(2)
    loop(1, 16, forward)
    ring_step(3)
    loop(0, 16, lambda d: pair_copy(d).wait())
    diagonal(first_ref, k_ref[0].reshape(BLK, BLK))
    arrive(panel_ref.at[:, pl.ds(1, 7)], got.at[4])
    ring_wait(0, 2, 1)
    ring_wait(1, 2, 0)
    ring_wait(0, 3, 0)
    ring_wait(1, 3, 1)

    loop(1, 16, lambda d: k_copy(d).wait_send())
    loop(1, 32, lambda d: child_copy(d).wait_send())

    @pl.when(has_front)
    def _():
        loop(1, 32, lambda d: front_copy(d).wait_send())
        loop(1, 32, lambda d: rest_copy(d).wait_send())

    for d in range(1, 4):
        map_copy(d).wait_send()
    for i in range(NPIV):
        @pl.when(r == i)
        def _():
            for d in range(1, 8):
                for copy in z_copies(i, d):
                    copy.wait_send()

    for hop in hops:
        ring_copy(*hop).wait_send()


def gather_all(child, front, child_map):
    dma = pltpu.SemaphoreType.DMA
    return pl.pallas_call(
        gather_kernel,
        out_shape=(
            jax.ShapeDtypeStruct((NTILE, 32, 4, BLK), jnp.float32),
            jax.ShapeDtypeStruct((4, 16, BLK), jnp.int32),
            jax.ShapeDtypeStruct((8, 32, 2, 2, 4, BLK), jnp.float32),
            jax.ShapeDtypeStruct((NPIV, 8, 4, BLK), jnp.float32),
            jax.ShapeDtypeStruct((BLK, 2 * BLK), jnp.float32),
        ),
        in_specs=[VM, pl.BlockSpec(memory_space=pltpu.HBM), SM],
        out_specs=(VM,) * 5,
        scratch_shapes=[
            pltpu.VMEM((32, 2, 2, 4, BLK), jnp.float32),
            pltpu.VMEM((1024, BLK), jnp.float32),
            pltpu.VMEM((8, 32, 4, BLK), jnp.float32),
            pltpu.VMEM((16, BLK), jnp.int32),
            pltpu.VMEM((NPIV, 30, 4, BLK), jnp.float32),
            pltpu.VMEM((NTILE, 4, BLK), jnp.float32),
            dma((9,)), dma((6,)), dma((NPIV,)), dma((NPIV,)), dma((16,)), dma((16,)), dma((2, 8)),
        ],
        compiler_params=pltpu.CompilerParams(collective_id=0, has_side_effects=True),
        name="gather_all",
    )(child, front, child_map)


def factor_kernel(
    k_ref, acc_ref, panel_ref, front_ref, first_ref, low_ref, inv_ref, rows_ref, moved_ref, top_ref,
    a_ref, m_ref, piece_ref, share_ref, w_ref, send, got, r_got, p_got, t_got,
):
    at = Place()
    r, c, s, e = at.r, at.c, at.s, at.e
    spot = jnp.minimum(r, NPIV - 1)

    def prepare():
        fetch = [pltpu.make_async_copy(acc_ref.at[4 * j, :, 0], piece_ref.at[j], got.at[2 + j]) for j in range(NPIV)]
        tiles = [
            pltpu.make_async_copy(
                k_ref.at[t], m_ref.at[pl.ds(i * BLK, BLK), pl.ds(j * BLK, BLK)], got.at[2 + NPIV + t]
            )
            for t, (i, j) in enumerate(TILES)
        ]
        for copy in fetch + tiles:
            copy.start()
        factor_begin(low_ref, m_ref)
        for copy in fetch:
            copy.wait()
        for j in range(NPIV):
            for slot in range(8):
                share_ref[slot, j] = piece_ref[j, slot] + panel_ref[j, slot]
        for copy in tiles:
            copy.wait()
        factor_finish(0, low_ref, inv_ref, first_ref, m_ref)

    at.greet(prepare)

    top_part, rest_part = pl.ds(0, 1), pl.ds(1, 7)

    def move_copy(d, part, k):
        p, device = at.plane(d)
        return push(acc_ref.at[p, part], moved_ref.at[part, :, e], send.at[4 * k], got.at[k * 29], device)

    def own_move(part, k):
        return pltpu.make_async_copy(acc_ref.at[e, part], moved_ref.at[part, :, e], got.at[k * 29])

    own_move(top_part, 0).start()
    loop(1, 32, lambda d: move_copy(d, top_part, 0).start())

    own_rows = pltpu.make_async_copy(share_ref, rows_ref.at[:, :, e], got.at[1])

    def rows_copy(d):
        return push(share_ref, rows_ref.at[:, :, e], send.at[1], r_got.at[d], at.same_core(d)[1])

    def pair_copy(d):
        where_e = at.same_core(16 - d)[0]
        return push(rows_ref.at[:, :, where_e], rows_ref.at[:, :, where_e], send.at[2], p_got.at[d], at.partner)

    def top_copy(d):
        return push(w_ref, top_ref.at[spot], send.at[3], t_got.at[spot], at.line(d))

    own_rows.start()
    loop(1, 16, lambda d: rows_copy(d).start())
    own_move(rest_part, 1).start()
    loop(1, 32, lambda d: move_copy(d, rest_part, 1).start())

    def after_first():
        own_rows.wait()
        pair_copy(0).start()
        arrive(moved_ref.at[top_part], got.at[0])

        @pl.when(r < NPIV)
        def _():
            for i in range(2):
                w_ref[i] = moved_ref[0, i] + front_ref[:BLK, i * BLK : (i + 1) * BLK].reshape(32, 4, BLK)
            pltpu.make_async_copy(w_ref, top_ref.at[spot], t_got.at[spot]).start()
            for d in (4, 3, 5, 2, 6, 1, 7):
                top_copy(d).start()

    def forward(d):
        rows_copy(d).wait_recv()
        pair_copy(d).start()

    def progress(b):
        pl.when(b == 2)(after_first)
        pl.when(b == 4)(lambda: loop(1, 16, forward))

    factor_steps(low_ref, inv_ref, a_ref, m_ref, progress)

    loop(0, 16, lambda d: pair_copy(d).wait())
    arrive(moved_ref.at[rest_part], got.at[29])
    for i in range(NPIV):
        arrive(top_ref.at[i], t_got.at[i])
    loop(1, 16, lambda d: rows_copy(d).wait_send())
    loop(1, 32, lambda d: move_copy(d, top_part, 0).wait_send())
    loop(1, 32, lambda d: move_copy(d, rest_part, 1).wait_send())

    @pl.when(r < NPIV)
    def _():
        for d in range(1, 8):
            top_copy(d).wait_send()


def factor_all(k, acc, panel, front, first):
    dma = pltpu.SemaphoreType.DMA
    f32 = lambda *shape: jax.ShapeDtypeStruct(shape, jnp.float32)
    return pl.pallas_call(
        factor_kernel,
        out_shape=(
            f32(PIV, PIV),
            f32(NPIV, BLK, BLK),
            f32(8, NPIV, 32, 4, BLK),
            f32(8, 2, 32, 4, BLK),
            f32(NPIV, 2, 32, 4, BLK),
        ),
        in_specs=[pl.BlockSpec(memory_space=pltpu.HBM)] * 2 + [VM] * 3,
        out_specs=(VM,) * 5,
        scratch_shapes=[
            pltpu.VMEM((BLK, 256), jnp.float32),
            pltpu.VMEM((PIV, PIV), jnp.float32),
            pltpu.VMEM((NPIV, 8, 4, BLK), jnp.float32),
            pltpu.VMEM((8, NPIV, 4, BLK), jnp.float32),
            pltpu.VMEM((2, 32, 4, BLK), jnp.float32),
            dma((5,)), dma((3 + NPIV + NTILE,)), dma((16,)), dma((16,)), dma((NPIV,)),
        ],
        compiler_params=pltpu.CompilerParams(collective_id=1, has_side_effects=True, vmem_limit_bytes=40 * 1024 * 1024),
        name="factor_all",
    )(k, acc, panel, front, first)


def place_kernel(map_ref, buf_ref, acc_ref):
    acc_ref[...] = jnp.zeros_like(acc_ref)
    row = lax.axis_index("row")

    for q in range(4):
        targets = [map_ref[q, j, 0] for j in range(16)]
        spots = [(j % 8 * 4 + j // 16, (j // 8) % 2) for j in targets]

        def child_row(block_row):
            i = map_ref[q, block_row, 0]

            @pl.when(i % 8 == row)
            def _():
                slot = i // 8
                for block_col, (dest, half) in enumerate(spots):
                    acc_ref[dest, slot, half] += buf_ref[
                        block_row % 8, block_col % 8 * 4 + q, block_row // 8, block_col // 8
                    ]

        loop(0, 16, child_row)


def place(maps, buf):
    return pl.pallas_call(
        place_kernel,
        out_shape=jax.ShapeDtypeStruct((32, 8, 2, 4, BLK), jnp.float32),
        in_specs=[SM, VM],
        out_specs=VM,
        name="place",
    )(maps, buf)


NT = ((1,), (1,))
NN = ((1,), (0,))


def four(a, b, c, d):
    return jnp.concatenate([jnp.concatenate([a, b], axis=1), jnp.concatenate([c, d], axis=1)], axis=0)


def schur_kernel(
    rows_ref, top_ref, moved_ref, front_ref, low_ref, inv_ref, out_ref,
    lh, ll, yh, yl, uh, ul, x_ref,
):
    row, col, sub = (lax.axis_index(a) for a in ("row", "col", "sub"))
    high, rest = split(low_ref[...])
    lh[...] = high
    ll[...] = rest
    zero = jnp.zeros((BLK, BLK), jnp.float32)
    for p in range(3):
        first, second = inv_ref[2 * p], inv_ref[2 * p + 1]
        at = 256 * p
        cross = jnp.dot(low_ref[at + BLK : at + 256, at : at + BLK], first, precision=HI)
        cross = -jnp.dot(second, cross, precision=HI)
        high, rest = split(four(first, zero, cross, second))
        yh[p] = high
        yl[p] = rest
    for p in range(3):
        at = 256 * p
        x = four(top_ref[2 * p, 0], top_ref[2 * p, 1], top_ref[2 * p + 1, 0], top_ref[2 * p + 1, 1])
        if p:
            x = x - dot3((lh[at : at + 256, :at], ll[at : at + 256, :at]), (uh[:at, :], ul[:at, :]), NN)
        high, rest = split(dot3((yh[p], yl[p]), split(x), NN))
        uh[at : at + 256, :] = high
        ul[at : at + 256, :] = rest

    def tile(t):
        here = pl.ds(pl.multiple_of(t * 256, 256), 256)
        a, b = 2 * t, 2 * t + 1
        acc = front_ref[here, :] + four(moved_ref[a, 0], moved_ref[a, 1], moved_ref[b, 0], moved_ref[b, 1])
        xs = []
        for p in range(3):
            at = 256 * p
            x = four(rows_ref[a, 2 * p], rows_ref[a, 2 * p + 1], rows_ref[b, 2 * p], rows_ref[b, 2 * p + 1])
            for m in range(p):
                cut = slice(256 * m, 256 * m + 256)
                x = x - dot3(xs[m], (lh[at : at + 256, cut], ll[at : at + 256, cut]), NT)
            x = dot3(split(x), (yh[p], yl[p]), NT)
            x_ref[here, at : at + 256] = x
            xs.append(split(x))
            acc = acc - dot3(xs[p], (uh[at : at + 256, :], ul[at : at + 256, :]), NN)
        out_ref[here, :] = acc

    loop(0, 4, tile)

    @pl.when(row < NPIV)
    def _():
        out_ref[:BLK, :] = jnp.zeros((BLK, 256), jnp.float32)
        x_ref[:BLK, :] = low_ref[pl.ds(pl.multiple_of(row * BLK, BLK), BLK), :]

    @pl.when((sub == 0) & (col < NPIV))
    def _():
        out_ref[:, :BLK] = x_ref[:, pl.ds(pl.multiple_of(col * BLK, BLK), BLK)]


def schur(rows, top, moved, front, low, inv):
    return pl.pallas_call(
        schur_kernel,
        out_shape=jax.ShapeDtypeStruct((1024, 256), jnp.float32),
        in_specs=[VM] * 6,
        out_specs=VM,
        scratch_shapes=[
            pltpu.VMEM((PIV, PIV), jnp.bfloat16),
            pltpu.VMEM((PIV, PIV), jnp.bfloat16),
            pltpu.VMEM((3, 256, 256), jnp.bfloat16),
            pltpu.VMEM((3, 256, 256), jnp.bfloat16),
            pltpu.VMEM((PIV, 256), jnp.bfloat16),
            pltpu.VMEM((PIV, 256), jnp.bfloat16),
            pltpu.VMEM((1024, PIV), jnp.float32),
        ],
        compiler_params=pltpu.CompilerParams(vmem_limit_bytes=32 * 1024 * 1024),
        name="schur",
    )(rows, top, moved, front, low, inv)


def body(front, child, child_map):
    k, maps, buf, panel, first = gather_all(child, front, child_map)
    acc = place(maps, buf)
    low, inv, rows, moved, top = factor_all(k.reshape(NTILE, BLK, BLK), acc, panel, front, first)
    return schur(
        rows.reshape(8, NPIV, BLK, BLK),
        top.reshape(NPIV, 2, BLK, BLK),
        moved.reshape(8, 2, BLK, BLK),
        front,
        low,
        inv,
    )


def solution(mesh):
    placed = (P("row", ("col", "sub")), P("sub", "row", "col"), P("sub", None))
    return jax.shard_map(
        body, mesh=mesh, in_specs=placed, out_specs=P("row", ("col", "sub")), check_vma=False
    )
```

profile of v0, /device:TPU:2, one launch (start us, length us, event | category | flops | bytes accessed | tf_op | source)
XLA Modules:
  0.0 117.6 jit_solution(7511135545564226302)
XLA Ops:
  0.0 0.0 copy-start
  0.0 49.2 %gather_all.1 = (f32[21,32,4,128]{3,2,1,0:T(4,128)}, s32[4,16,128]{2,1,0:T(8,128)}, f32[8,32,2,2,4,128]{5,4,3,2,1,0:T(4,128)}, f32[6,8,4,128]{3,2,1,0:T(4,128)}, f32[128,256]{1,0:T(8,128)}) custom-call(f32[1,256,256]{2,1,0:T(8,128)} %tile_ref.1, f32[1024,256]{1,0:T(8,128)} %front_ref.3, s32[1,16]{1,0:T(1,128)} %list_ref.1), custom_call_target="tpu_custom_call" | custom-call | tf_op jit(solution)/shard_map/gather_all/pallas_call | solution.py:372
  49.2 0.0 copy-start.2
  49.2 0.0 copy-start.3
  49.2 0.0 copy-start.4
  49.2 5.2 %place.1.acc_ref = f32[32,8,2,4,128]{4,3,2,1,0:T(4,128)} custom-call(s32[4,16,128]{2,1,0:T(8,128)} %get-tuple-element.16.map_ref, f32[8,32,2,2,4,128]{5,4,3,2,1,0:T(4,128)} %get-tuple-element.17.buf_ref), custom_call_target="tpu_custom_call" | custom-call | tf_op jit(solution)/shard_map/place/pallas_call | solution.py:543
  54.4 0.0 copy-done
  54.4 0.0 copy-done.2
  54.4 0.0 copy-done.3
  54.4 0.0 copy-done.4
  54.5 0.0 copy-start.1
  54.5 1.2 %copy-done.1 = f32[32,8,2,4,128]{4,3,2,1,0:T(4,128)S(1)} copy-done((f32[32,8,2,4,128]{4,3,2,1,0:T(4,128)S(1)}, f32[32,8,2,4,128]{4,3,2,1,0:T(4,128)}, u32[]{:S(2)}) %copy-start.1) | copy-done | bytes 1048600
  55.7 50.5 %factor_all.1 = (f32[768,768]{1,0:T(8,128)S(1)}, f32[6,128,128]{2,1,0:T(8,128)S(1)}, f32[8,6,32,4,128]{4,3,2,1,0:T(4,128)S(1)}, f32[8,2,32,4,128]{4,3,2,1,0:T(4,128)S(1)}, f32[6,2,32,4,128]{4,3,2,1,0:T(4,128)S(1)}) custom-call(f32[21,128,128]{2,1,0:T(8,128)S(1)} %bitcast.5, f32[32,8,2,4,128]{4,3,2,1,0:T(4,128)S(1)} %copy-done.1, ...), custom_call_target="tpu_custom_call" | custom-call | tf_op jit(solution)/shard_map/factor_all/pallas_call | solution.py:496
  106.1 11.4 %schur.1 = f32[1024,256]{1,0:T(8,128)} custom-call(f32[8,6,128,128]{3,2,1,0:T(8,128)S(1)} %bitcast.4, f32[6,2,128,128]{3,2,1,0:T(8,128)S(1)} %bitcast.7, f32[8,2,128,128]{3,2,1,0:T(8,128)S(1)} %bitcast.6, f32[1024,256]{1,0:T(8,128)S(1)} %copy-done, f32[768,768]{1,0:T(8,128)S(1)} %get-tuple-element.23.low_ref, f32[6,128,128]{2,1,0:T(8,128)S(1)} %get-tuple-element.24.inv_ref), custom_call_target="tpu_custom_call" | custom-call | tf_op jit(solution)/shard_map/schur/pallas_call | solution.py:616
Async XLA Ops:
  0.0 54.4 %copy-start = (f32[1024,256]{1,0:T(8,128)S(1)}, f32[1024,256]{1,0:T(8,128)}, u32[]{:S(2)}) copy-start(f32[1024,256]{1,0:T(8,128)} %front_ref.3) | copy-start | bytes 3145732
  49.2 5.2 %copy-start.2 = (f32[21,32,4,128]{3,2,1,0:T(4,128)S(1)}, f32[21,32,4,128]{3,2,1,0:T(4,128)}, u32[]{:S(2)}) copy-start(f32[21,32,4,128]{3,2,1,0:T(4,128)} %get-tuple-element.15) | copy-start | bytes 4128772
  49.2 5.2 %copy-start.3 = (f32[128,256]{1,0:T(8,128)S(1)}, f32[128,256]{1,0:T(8,128)}, u32[]{:S(2)}) copy-start(f32[128,256]{1,0:T(8,128)} %get-tuple-element.19.first_ref) | copy-start | bytes 393220
  49.2 5.2 %copy-start.4 = (f32[6,8,4,128]{3,2,1,0:T(4,128)S(1)}, f32[6,8,4,128]{3,2,1,0:T(4,128)}, u32[]{:S(2)}) copy-start(f32[6,8,4,128]{3,2,1,0:T(4,128)} %get-tuple-element.18.panel_ref) | copy-start | bytes 294916
  54.5 1.2 %copy-start.1 = (f32[32,8,2,4,128]{4,3,2,1,0:T(4,128)S(1)}, f32[32,8,2,4,128]{4,3,2,1,0:T(4,128)}, u32[]{:S(2)}) copy-start(f32[32,8,2,4,128]{4,3,2,1,0:T(4,128)} %place.1.acc_ref) | copy-start | bytes 3145732
where the time goes:
time: 118 us
  Pallas kernels  116 us (98%)
  local copies, waits for them, and re-layouts  1.24 us (1%)
    pallas_call x1, Pallas kernels, factor_all(): pl.pallas_call(factor_kernel, out_shape=(f32(PIV, PIV), f32(NPIV, BLK, BL...  50.5 us
    pallas_call x1, Pallas kernels, gather_all(): pl.pallas_call(gather_kernel, out_shape=(jax.ShapeDtypeStruct((NTILE, 32,...  49.2 us
    pallas_call x1, Pallas kernels, schur(): pl.pallas_call(schur_kernel, out_shape=jax.ShapeDtypeStruct((1024, 256),...  11.4 us
    pallas_call x1, Pallas kernels, place(): pl.pallas_call(place_kernel, out_shape=jax.ShapeDtypeStruct((32, 8, 2, 4,...  5.21 us

commit v1 on v0

--- a/solution.py
+++ b/solution.py
@@ -220,9 +220,12 @@
     at.greet(prepare)
     seat = jnp.minimum(c, NPIV - 1)
 
-    def child_copy(d):
+    def child_copy(d, h):
         p, device = at.plane(d)
-        return push(child_ref.at[p], buf_ref.at[r, e], send.at[0], got.at[0], device)
+        return push(child_ref.at[p, h], buf_ref.at[r, e, h], send.at[9 * h], got.at[6 * h], device)
+
+    def own_child(h):
+        return pltpu.make_async_copy(child_ref.at[e, h], buf_ref.at[r, e, h], got.at[6 * h])
 
     def front_copy(d):
         p, device = at.plane(d)
@@ -235,9 +238,10 @@
     def map_copy(d):
         return push(map_ref, maps_ref.at[s], send.at[2], got.at[2], (r, c, (s + d) % 4))
 
-    pltpu.make_async_copy(child_ref.at[e], buf_ref.at[r, e], got.at[0]).start()
+    own_child(0).start()
+    own_child(1).start()
     pltpu.make_async_copy(map_ref, maps_ref.at[s], got.at[2]).start()
-    loop(1, 32, lambda d: child_copy(d).start())
+    loop(1, 32, lambda d: child_copy(d, 0).start())
 
     @pl.when(has_front)
     def _():
@@ -246,6 +250,7 @@
 
     for d in range(1, 4):
         map_copy(d).start()
+    loop(1, 32, lambda d: child_copy(d, 1).start())
 
     def z_copies(i, d):
         device = at.line(d)
@@ -271,9 +276,11 @@
             if hop[1] == k:
                 if k:
                     ring_wait(hop[0], k - 1, hop[2])
+                elif hop == (0, 0, 1):
+                    arrive(buf_ref.at[r, :, 1], got.at[6])
                 ring_copy(*hop).start()
 
-    arrive(buf_ref.at[r], got.at[0])
+    arrive(buf_ref.at[r, :, 0], got.at[0])
     arrive(panel_ref.at[:, 0], got.at[1])
 
     for i in range(NPIV):
@@ -347,7 +354,8 @@
     ring_wait(1, 3, 1)
 
     loop(1, 16, lambda d: k_copy(d).wait_send())
-    loop(1, 32, lambda d: child_copy(d).wait_send())
+    loop(1, 32, lambda d: child_copy(d, 0).wait_send())
+    loop(1, 32, lambda d: child_copy(d, 1).wait_send())
 
     @pl.when(has_front)
     def _():
@@ -387,9 +395,9 @@
             pltpu.VMEM((16, BLK), jnp.int32),
             pltpu.VMEM((NPIV, 30, 4, BLK), jnp.float32),
             pltpu.VMEM((NTILE, 4, BLK), jnp.float32),
-            dma((9,)), dma((6,)), dma((NPIV,)), dma((NPIV,)), dma((16,)), dma((16,)), dma((2, 8)),
+            dma((10,)), dma((7,)), dma((NPIV,)), dma((NPIV,)), dma((16,)), dma((16,)), dma((2, 8)),
         ],
-        compiler_params=pltpu.CompilerParams(collective_id=0, has_side_effects=True),
+        compiler_params=pltpu.CompilerParams(collective_id=0, has_side_effects=True, vmem_limit_bytes=20 * 1024 * 1024),
         name="gather_all",
     )(child, front, child_map)
 
@@ -545,6 +553,7 @@
         out_shape=jax.ShapeDtypeStruct((32, 8, 2, 4, BLK), jnp.float32),
         in_specs=[SM, VM],
         out_specs=VM,
+        compiler_params=pltpu.CompilerParams(vmem_limit_bytes=8 * 1024 * 1024),
         name="place",
     )(maps, buf)
 
@@ -583,24 +592,22 @@
         uh[at : at + 256, :] = high
         ul[at : at + 256, :] = rest
 
-    def tile(t):
-        here = pl.ds(pl.multiple_of(t * 256, 256), 256)
-        a, b = 2 * t, 2 * t + 1
-        acc = front_ref[here, :] + four(moved_ref[a, 0], moved_ref[a, 1], moved_ref[b, 0], moved_ref[b, 1])
-        xs = []
-        for p in range(3):
-            at = 256 * p
-            x = four(rows_ref[a, 2 * p], rows_ref[a, 2 * p + 1], rows_ref[b, 2 * p], rows_ref[b, 2 * p + 1])
-            for m in range(p):
-                cut = slice(256 * m, 256 * m + 256)
-                x = x - dot3(xs[m], (lh[at : at + 256, cut], ll[at : at + 256, cut]), NT)
-            x = dot3(split(x), (yh[p], yl[p]), NT)
-            x_ref[here, at : at + 256] = x
-            xs.append(split(x))
-            acc = acc - dot3(xs[p], (uh[at : at + 256, :], ul[at : at + 256, :]), NN)
-        out_ref[here, :] = acc
-
-    loop(0, 4, tile)
+    def stack(get):
+        return jnp.concatenate([jnp.concatenate([get(i, 0), get(i, 1)], axis=1) for i in range(8)], axis=0)
+
+    acc = front_ref[...] + stack(lambda i, j: moved_ref[i, j])
+    xs = []
+    for p in range(3):
+        at = 256 * p
+        x = stack(lambda i, j: rows_ref[i, 2 * p + j])
+        for m in range(p):
+            cut = slice(256 * m, 256 * m + 256)
+            x = x - dot3(xs[m], (lh[at : at + 256, cut], ll[at : at + 256, cut]), NT)
+        x = dot3(split(x), (yh[p], yl[p]), NT)
+        x_ref[:, at : at + 256] = x
+        xs.append(split(x))
+        acc = acc - dot3(xs[p], (uh[at : at + 256, :], ul[at : at + 256, :]), NN)
+    out_ref[...] = acc
 
     @pl.when(row < NPIV)
     def _():

time: 118 us -> 112 us (0.949)
  Pallas kernels: 116 us -> 108 us
  local copies, waits for them, and re-layouts: 1.24 us -> 2.83 us
    pallas_call x1, Pallas kernels: 11.4 us -> 7.91 us  [schur(): pl.pallas_call(schur_kernel, out_shape=jax.ShapeDtypeStruct((1024, 256),...]
    pallas_call x1, Pallas kernels: 49.2 us -> 46.8 us  [gather_all(): pl.pallas_call(gather_kernel, out_shape=(jax.ShapeDtypeStruct((NTILE, 32,...]
    unnamed x10 -> x8, local copies, waits for them, and re-layouts: 1.24 us -> 2.83 us
    pallas_call x1, Pallas kernels: 5.21 us -> 3.91 us  [place(): pl.pallas_call(place_kernel, out_shape=jax.ShapeDtypeStruct((32, 8, 2, 4,...]
where the time goes in v1:
time: 112 us; the launch traced here: 111 us
  Pallas kernels  108 us (96%)
  local copies, waits for them, and re-layouts  2.83 us (3%)
    pallas_call x1, Pallas kernels, factor_all(): pl.pallas_call(factor_kernel, out_shape=(f32(PIV, PIV), f32(NPIV, BLK, BL...  49.8 us
    pallas_call x1, Pallas kernels, gather_all(): pl.pallas_call(gather_kernel, out_shape=(jax.ShapeDtypeStruct((NTILE, 32,...  46.8 us
    pallas_call x1, Pallas kernels, schur(): pl.pallas_call(schur_kernel, out_shape=jax.ShapeDtypeStruct((1024, 256),...  7.91 us
    pallas_call x1, Pallas kernels, place(): pl.pallas_call(place_kernel, out_shape=jax.ShapeDtypeStruct((32, 8, 2, 4,...  3.91 us
    unnamed x8, local copies, waits for them, and re-layouts  2.83 us

profile of v1, /device:TPU:2, one launch (start us, length us, event | category | flops | bytes accessed | tf_op | source)
XLA Modules:
  0.0 111.3 jit_solution(16936759276483320823)
XLA Ops:
  0.0 0.0 copy-start
  0.0 1.2 %copy-done = f32[1024,256]{1,0:T(8,128)S(1)} copy-done((f32[1024,256]{1,0:T(8,128)S(1)}, f32[1024,256]{1,0:T(8,128)}, u32[]{:S(2)}) %copy-start) | copy-done | bytes 1048600
  1.2 0.0 copy-start.2
  1.2 0.9 copy-done.2
  2.2 0.0 copy-start.3
  2.2 0.7 copy-done.3
  2.8 0.0 copy-start.1
  2.8 46.8 %gather_all.1 = (f32[21,32,4,128]{3,2,1,0:T(4,128)S(1)}, s32[4,16,128]{2,1,0:T(8,128)S(1)}, f32[8,32,2,2,4,128]{5,4,3,2,1,0:T(4,128)S(1)}, f32[6,8,4,128]{3,2,1,0:T(4,128)S(1)}, f32[128,256]{1,0:T(8,128)S(1)}) custom-call(f32[1,256,256]{2,1,0:T(8,128)S(1)} %copy-done.2, f32[1024,256]{1,0:T(8,128)S(1)} %copy-done, s32[1,16]{1,0:T(1,128)S(1)} %copy-done.3), custom_call_target="tpu_custom_call" | custom-call | tf_op jit(solution)/shard_map/gather_all/pallas_call | solution.py:380
  49.7 3.9 %place.1.acc_ref = f32[32,8,2,4,128]{4,3,2,1,0:T(4,128)S(1)} custom-call(s32[4,16,128]{2,1,0:T(8,128)S(1)} %get-tuple-element.16.map_ref, f32[8,32,2,2,4,128]{5,4,3,2,1,0:T(4,128)S(1)} %get-tuple-element.17.buf_ref), custom_call_target="tpu_custom_call" | custom-call | tf_op jit(solution)/shard_map/place/pallas_call | solution.py:551
  53.6 0.0 copy-done.1
  53.6 49.8 %factor_all.1 = (f32[768,768]{1,0:T(8,128)S(1)}, f32[6,128,128]{2,1,0:T(8,128)S(1)}, f32[8,6,32,4,128]{4,3,2,1,0:T(4,128)S(1)}, f32[8,2,32,4,128]{4,3,2,1,0:T(4,128)S(1)}, f32[6,2,32,4,128]{4,3,2,1,0:T(4,128)S(1)}) custom-call(f32[21,128,128]{2,1,0:T(8,128)S(1)} %bitcast.5, f32[32,8,2,4,128]{4,3,2,1,0:T(4,128)S(1)} %place.1.acc_ref, ...), custom_call_target="tpu_custom_call" | custom-call | tf_op jit(solution)/shard_map/factor_all/pallas_call | solution.py:504
  103.4 7.9 %schur.1 = f32[1024,256]{1,0:T(8,128)} custom-call(f32[8,6,128,128]{3,2,1,0:T(8,128)S(1)} %bitcast.4, f32[6,2,128,128]{3,2,1,0:T(8,128)S(1)} %bitcast.7, f32[8,2,128,128]{3,2,1,0:T(8,128)S(1)} %bitcast.6, f32[1024,256]{1,0:T(8,128)S(1)} %copy-done.1, f32[768,768]{1,0:T(8,128)S(1)} %get-tuple-element.23.low_ref, f32[6,128,128]{2,1,0:T(8,128)S(1)} %get-tuple-element.24.inv_ref), custom_call_target="tpu_custom_call" | custom-call | tf_op jit(solution)/shard_map/schur/pallas_call | solution.py:623
Async XLA Ops:
  0.0 1.2 %copy-start = (f32[1024,256]{1,0:T(8,128)S(1)}, f32[1024,256]{1,0:T(8,128)}, u32[]{:S(2)}) copy-start(f32[1024,256]{1,0:T(8,128)} %front_ref.3) | copy-start | bytes 3145732
  1.2 0.9 copy-start.2
  2.2 0.7 copy-start.3
  2.8 50.8 %copy-start.1 = (f32[1024,256]{1,0:T(8,128)S(1)}, f32[1024,256]{1,0:T(8,128)}, u32[]{:S(2)}) copy-start(f32[1024,256]{1,0:T(8,128)} %front_ref.3) | copy-start | bytes 3145732

commit v2 on v1

--- a/solution.py
+++ b/solution.py
@@ -108,7 +108,7 @@
 
     def solve(i, c):
         rows = pl.ds(pl.multiple_of(i * BLK, BLK), BLK)
-        l_ref[rows, at] = nt(m_ref[rows, at], y)
+        l_ref[rows, at] = nt3(m_ref[rows, at], y)
         return c
 
     lax.fori_loop(b + 1, NPIV, solve, 0)
@@ -193,8 +193,8 @@
 
 
 def gather_kernel(
-    tile_ref, whole_ref, list_ref, k_ref, maps_ref, buf_ref, panel_ref, first_ref,
-    child_ref, strip_ref, front_ref, map_ref, z_ref, acc_ref, send, got, z_got, f_got, k_got, p_got, ring_got,
+    child_hbm, whole_ref, list_ref, k_ref, maps_ref, buf_ref, panel_ref, first_ref,
+    tile_ref, child_ref, strip_ref, front_ref, map_ref, z_ref, acc_ref, send, got, z_got, f_got, k_got, p_got, ring_got,
 ):
     at = Place()
     r, c, s, e = at.r, at.c, at.s, at.e
@@ -203,13 +203,16 @@
     def prepare():
         fetch = pltpu.make_async_copy(whole_ref.at[:, pl.ds(0, BLK)], strip_ref, got.at[5])
         fetch.start()
-        for i in range(2):
-            for j in range(2):
-                child_ref[:, i, j] = tile_ref[0, i * BLK : (i + 1) * BLK, j * BLK : (j + 1) * BLK].reshape(32, 4, BLK)
+        child_fetch = pltpu.make_async_copy(child_hbm.at[0], tile_ref, got.at[7])
+        child_fetch.start()
         for i in range(16):
             map_ref[i : i + 1, :] = jnp.full((1, BLK), list_ref[0, i], jnp.int32)
         for i in range(NPIV - 1):
             z_ref[i, 4 * (i + 1) : 24] = jnp.zeros((20 - 4 * i, 4, BLK), jnp.float32)
+        child_fetch.wait()
+        for i in range(2):
+            for j in range(2):
+                child_ref[:, i, j] = tile_ref[i * BLK : (i + 1) * BLK, j * BLK : (j + 1) * BLK].reshape(32, 4, BLK)
         fetch.wait()
 
         @pl.when(has_front)
@@ -386,16 +389,17 @@
             jax.ShapeDtypeStruct((NPIV, 8, 4, BLK), jnp.float32),
             jax.ShapeDtypeStruct((BLK, 2 * BLK), jnp.float32),
         ),
-        in_specs=[VM, pl.BlockSpec(memory_space=pltpu.HBM), SM],
+        in_specs=[pl.BlockSpec(memory_space=pltpu.HBM)] * 2 + [SM],
         out_specs=(VM,) * 5,
         scratch_shapes=[
+            pltpu.VMEM((256, 256), jnp.float32),
             pltpu.VMEM((32, 2, 2, 4, BLK), jnp.float32),
             pltpu.VMEM((1024, BLK), jnp.float32),
             pltpu.VMEM((8, 32, 4, BLK), jnp.float32),
             pltpu.VMEM((16, BLK), jnp.int32),
             pltpu.VMEM((NPIV, 30, 4, BLK), jnp.float32),
             pltpu.VMEM((NTILE, 4, BLK), jnp.float32),
-            dma((10,)), dma((7,)), dma((NPIV,)), dma((NPIV,)), dma((16,)), dma((16,)), dma((2, 8)),
+            dma((10,)), dma((8,)), dma((NPIV,)), dma((NPIV,)), dma((16,)), dma((16,)), dma((2, 8)),
         ],
         compiler_params=pltpu.CompilerParams(collective_id=0, has_side_effects=True, vmem_limit_bytes=20 * 1024 * 1024),
         name="gather_all",
@@ -640,7 +644,11 @@
 
 
 def body(front, child, child_map):
-    k, maps, buf, panel, first = gather_all(child, front, child_map)
+    k, maps, buf, panel, first = gather_all(
+        pltpu.with_memory_space_constraint(child, pltpu.HBM),
+        pltpu.with_memory_space_constraint(front, pltpu.HBM),
+        child_map,
+    )
     acc = place(maps, buf)
     low, inv, rows, moved, top = factor_all(k.reshape(NTILE, BLK, BLK), acc, panel, front, first)
     return schur(

time: 112 us -> 110 us (0.982)
  local copies, waits for them, and re-layouts: 2.83 us -> 0.75 us
    unnamed x8 -> x4, local copies, waits for them, and re-layouts: 2.83 us -> 0.75 us
where the time goes in v2:
time: 110 us; the launch traced here: 109 us
  Pallas kernels  108 us (98%)
    pallas_call x1, Pallas kernels, factor_all(): pl.pallas_call(factor_kernel, out_shape=(f32(PIV, PIV), f32(NPIV, BLK, BL...  49.9 us
    pallas_call x1, Pallas kernels, gather_all(): pl.pallas_call(gather_kernel, out_shape=(jax.ShapeDtypeStruct((NTILE, 32,...  46.8 us
    pallas_call x1, Pallas kernels, schur(): pl.pallas_call(schur_kernel, out_shape=jax.ShapeDtypeStruct((1024, 256),...  7.91 us
    pallas_call x1, Pallas kernels, place(): pl.pallas_call(place_kernel, out_shape=jax.ShapeDtypeStruct((32, 8, 2, 4,...  3.66 us

profile of v2, /device:TPU:2, one launch (start us, length us, event | category | flops | bytes accessed | tf_op | source)
XLA Modules:
  0.0 109.1 jit_solution(8778088609657337992)
XLA Ops:
  0.0 0.0 copy-start
  0.0 0.0 copy-start.1
  0.0 0.7 copy-done.1
  0.7 46.8 %gather_all.1 = (f32[21,32,4,128]{3,2,1,0:T(4,128)S(1)}, s32[4,16,128]{2,1,0:T(8,128)S(1)}, f32[8,32,2,2,4,128]{5,4,3,2,1,0:T(4,128)S(1)}, f32[6,8,4,128]{3,2,1,0:T(4,128)S(1)}, f32[128,256]{1,0:T(8,128)S(1)}) custom-call(f32[1,256,256]{2,1,0:T(8,128)} %child_hbm.1, f32[1024,256]{1,0:T(8,128)} %front_ref.3, s32[1,16]{1,0:T(1,128)S(1)} %copy-done.1), custom_call_target="tpu_custom_call" | custom-call | tf_op jit(solution)/shard_map/gather_all/pallas_call | solution.py:383
  47.6 3.7 %place.1.acc_ref = f32[32,8,2,4,128]{4,3,2,1,0:T(4,128)S(1)} custom-call(s32[4,16,128]{2,1,0:T(8,128)S(1)} %get-tuple-element.16.map_ref, f32[8,32,2,2,4,128]{5,4,3,2,1,0:T(4,128)S(1)} %get-tuple-element.17.buf_ref), custom_call_target="tpu_custom_call" | custom-call | tf_op jit(solution)/shard_map/place/pallas_call | solution.py:555
  51.3 0.0 copy-done
  51.3 49.9 %factor_all.1 = (f32[768,768]{1,0:T(8,128)S(1)}, f32[6,128,128]{2,1,0:T(8,128)S(1)}, f32[8,6,32,4,128]{4,3,2,1,0:T(4,128)S(1)}, f32[8,2,32,4,128]{4,3,2,1,0:T(4,128)S(1)}, f32[6,2,32,4,128]{4,3,2,1,0:T(4,128)S(1)}) custom-call(f32[21,128,128]{2,1,0:T(8,128)S(1)} %bitcast.5, f32[32,8,2,4,128]{4,3,2,1,0:T(4,128)S(1)} %place.1.acc_ref, ...), custom_call_target="tpu_custom_call" | custom-call | tf_op jit(solution)/shard_map/factor_all/pallas_call | solution.py:508
  101.2 7.9 %schur.1 = f32[1024,256]{1,0:T(8,128)} custom-call(f32[8,6,128,128]{3,2,1,0:T(8,128)S(1)} %bitcast.4, f32[6,2,128,128]{3,2,1,0:T(8,128)S(1)} %bitcast.7, f32[8,2,128,128]{3,2,1,0:T(8,128)S(1)} %bitcast.6, f32[1024,256]{1,0:T(8,128)S(1)} %copy-done, f32[768,768]{1,0:T(8,128)S(1)} %get-tuple-element.23.low_ref, f32[6,128,128]{2,1,0:T(8,128)S(1)} %get-tuple-element.24.inv_ref), custom_call_target="tpu_custom_call" | custom-call | tf_op jit(solution)/shard_map/schur/pallas_call | solution.py:627
Async XLA Ops:
  0.0 51.3 %copy-start = (f32[1024,256]{1,0:T(8,128)S(1)}, f32[1024,256]{1,0:T(8,128)}, u32[]{:S(2)}) copy-start(f32[1024,256]{1,0:T(8,128)} %front_ref.3) | copy-start | bytes 3145732
  0.0 0.7 copy-start.1

commit v3 on v2

--- a/solution.py
+++ b/solution.py
@@ -106,16 +106,20 @@
     y_ref[b] = y
     l_ref[at, at] = jnp.where(r_iota >= c_iota, a_ref[:, :BLK].T, 0.0)
 
+    ys = split(y)
+
     def solve(i, c):
         rows = pl.ds(pl.multiple_of(i * BLK, BLK), BLK)
-        l_ref[rows, at] = nt3(m_ref[rows, at], y)
+        l_ref[rows, at] = dot3(split(m_ref[rows, at]), ys, ((1,), (1,)))
         return c
 
     lax.fori_loop(b + 1, NPIV, solve, 0)
+
+    column = split(l_ref[:, at])
 
     def update(i, c):
         rows = pl.ds(pl.multiple_of(i * BLK, BLK), BLK)
-        m_ref[rows, :] = m_ref[rows, :] - nt3(l_ref[rows, at], l_ref[:, at])
+        m_ref[rows, :] = m_ref[rows, :] - dot3(split(l_ref[rows, at]), column, ((1,), (1,)))
         return c
 
     lax.fori_loop(b + 1, NPIV, update, 0)
@@ -193,8 +197,8 @@
 
 
 def gather_kernel(
-    child_hbm, whole_ref, list_ref, k_ref, maps_ref, buf_ref, panel_ref, first_ref,
-    tile_ref, child_ref, strip_ref, front_ref, map_ref, z_ref, acc_ref, send, got, z_got, f_got, k_got, p_got, ring_got,
+    child_hbm, whole_ref, list_hbm, k_ref, maps_ref, buf_ref, panel_ref, first_ref,
+    list_ref, tile_ref, child_ref, strip_ref, front_ref, map_ref, z_ref, acc_ref, send, got, z_got, f_got, k_got, p_got, ring_got,
 ):
     at = Place()
     r, c, s, e = at.r, at.c, at.s, at.e
@@ -205,6 +209,9 @@
         fetch.start()
         child_fetch = pltpu.make_async_copy(child_hbm.at[0], tile_ref, got.at[7])
         child_fetch.start()
+        list_fetch = pltpu.make_async_copy(list_hbm, list_ref, got.at[8])
+        list_fetch.start()
+        list_fetch.wait()
         for i in range(16):
             map_ref[i : i + 1, :] = jnp.full((1, BLK), list_ref[0, i], jnp.int32)
         for i in range(NPIV - 1):
@@ -389,9 +396,10 @@
             jax.ShapeDtypeStruct((NPIV, 8, 4, BLK), jnp.float32),
             jax.ShapeDtypeStruct((BLK, 2 * BLK), jnp.float32),
         ),
-        in_specs=[pl.BlockSpec(memory_space=pltpu.HBM)] * 2 + [SM],
+        in_specs=[pl.BlockSpec(memory_space=pltpu.HBM)] * 3,
         out_specs=(VM,) * 5,
         scratch_shapes=[
+            pltpu.SMEM((1, 16), jnp.int32),
             pltpu.VMEM((256, 256), jnp.float32),
             pltpu.VMEM((32, 2, 2, 4, BLK), jnp.float32),
             pltpu.VMEM((1024, BLK), jnp.float32),
@@ -399,7 +407,7 @@
             pltpu.VMEM((16, BLK), jnp.int32),
             pltpu.VMEM((NPIV, 30, 4, BLK), jnp.float32),
             pltpu.VMEM((NTILE, 4, BLK), jnp.float32),
-            dma((10,)), dma((8,)), dma((NPIV,)), dma((NPIV,)), dma((16,)), dma((16,)), dma((2, 8)),
+            dma((10,)), dma((9,)), dma((NPIV,)), dma((NPIV,)), dma((16,)), dma((16,)), dma((2, 8)),
         ],
         compiler_params=pltpu.CompilerParams(collective_id=0, has_side_effects=True, vmem_limit_bytes=20 * 1024 * 1024),
         name="gather_all",
@@ -647,7 +655,7 @@
     k, maps, buf, panel, first = gather_all(
         pltpu.with_memory_space_constraint(child, pltpu.HBM),
         pltpu.with_memory_space_constraint(front, pltpu.HBM),
-        child_map,
+        pltpu.with_memory_space_constraint(child_map, pltpu.HBM),
     )
     acc = place(maps, buf)
     low, inv, rows, moved, top = factor_all(k.reshape(NTILE, BLK, BLK), acc, panel, front, first)

time: 110 us -> 108 us (0.982)
  no operation moved by 1% of the time
where the time goes in v3:
time: 108 us
  Pallas kernels  108 us (100%)
    pallas_call x1, Pallas kernels, factor_all(): pl.pallas_call(factor_kernel, out_shape=(f32(PIV, PIV), f32(NPIV, BLK, BL...  49.9 us
    pallas_call x1, Pallas kernels, gather_all(): pl.pallas_call(gather_kernel, out_shape=(jax.ShapeDtypeStruct((NTILE, 32,...  46.1 us
    pallas_call x1, Pallas kernels, schur(): pl.pallas_call(schur_kernel, out_shape=jax.ShapeDtypeStruct((1024, 256),...  7.91 us
    pallas_call x1, Pallas kernels, place(): pl.pallas_call(place_kernel, out_shape=jax.ShapeDtypeStruct((32, 8, 2, 4,...  4.04 us

profile of v3, /device:TPU:2, one launch (start us, length us, event | category | flops | bytes accessed | tf_op | source)
XLA Modules:
  0.0 108.0 jit_solution(13517745424958091883)
XLA Ops:
  0.0 0.0 copy-start
  0.0 46.1 %gather_all.1 = (f32[21,32,4,128]{3,2,1,0:T(4,128)S(1)}, s32[4,16,128]{2,1,0:T(8,128)S(1)}, f32[8,32,2,2,4,128]{5,4,3,2,1,0:T(4,128)S(1)}, f32[6,8,4,128]{3,2,1,0:T(4,128)S(1)}, f32[128,256]{1,0:T(8,128)S(1)}) custom-call(f32[1,256,256]{2,1,0:T(8,128)} %child_hbm.1, f32[1024,256]{1,0:T(8,128)} %front_ref.3, s32[1,16]{1,0:T(1,128)} %list_hbm.1), custom_call_target="tpu_custom_call" | custom-call | tf_op jit(solution)/shard_map/gather_all/pallas_call | solution.py:390
  46.2 4.0 %place.1.acc_ref = f32[32,8,2,4,128]{4,3,2,1,0:T(4,128)S(1)} custom-call(s32[4,16,128]{2,1,0:T(8,128)S(1)} %get-tuple-element.16.map_ref, f32[8,32,2,2,4,128]{5,4,3,2,1,0:T(4,128)S(1)} %get-tuple-element.17.buf_ref), custom_call_target="tpu_custom_call" | custom-call | tf_op jit(solution)/shard_map/place/pallas_call | solution.py:563
  50.2 0.0 copy-done
  50.2 49.9 %factor_all.1 = (f32[768,768]{1,0:T(8,128)S(1)}, f32[6,128,128]{2,1,0:T(8,128)S(1)}, f32[8,6,32,4,128]{4,3,2,1,0:T(4,128)S(1)}, f32[8,2,32,4,128]{4,3,2,1,0:T(4,128)S(1)}, f32[6,2,32,4,128]{4,3,2,1,0:T(4,128)S(1)}) custom-call(f32[21,128,128]{2,1,0:T(8,128)S(1)} %bitcast.5, f32[32,8,2,4,128]{4,3,2,1,0:T(4,128)S(1)} %place.1.acc_ref, ...), custom_call_target="tpu_custom_call" | custom-call | tf_op jit(solution)/shard_map/factor_all/pallas_call | solution.py:516
  100.1 7.9 %schur.1 = f32[1024,256]{1,0:T(8,128)} custom-call(f32[8,6,128,128]{3,2,1,0:T(8,128)S(1)} %bitcast.4, f32[6,2,128,128]{3,2,1,0:T(8,128)S(1)} %bitcast.7, f32[8,2,128,128]{3,2,1,0:T(8,128)S(1)} %bitcast.6, f32[1024,256]{1,0:T(8,128)S(1)} %copy-done, f32[768,768]{1,0:T(8,128)S(1)} %get-tuple-element.23.low_ref, f32[6,128,128]{2,1,0:T(8,128)S(1)} %get-tuple-element.24.inv_ref), custom_call_target="tpu_custom_call" | custom-call | tf_op jit(solution)/shard_map/schur/pallas_call | solution.py:635
Async XLA Ops:
  0.0 50.2 %copy-start = (f32[1024,256]{1,0:T(8,128)S(1)}, f32[1024,256]{1,0:T(8,128)}, u32[]{:S(2)}) copy-start(f32[1024,256]{1,0:T(8,128)} %front_ref.3) | copy-start | bytes 3145732
